TPU v7x, 128 devices: a whole 4x4x4 slice. The times are simulated.
128 devices in a mesh: dp: 4 (over x), fsdp: 32 (over z, y, core).
Axes of the slice: x: 4, y: 4, z: 4, core: 2. Of those that a mesh axis runs over, the one named last changes fastest.
Arguments:
- mlp_input: bfloat16 [1024, 4096], P('dp', 'fsdp'), may hold values from -6 to 6
- residual_in: bfloat16 [1024, 4096], P(('dp', 'fsdp')), may hold values from -6 to 6
- gate_weight: bfloat16 [4096, 14336], P(None, 'fsdp'), may hold values from -0.09375 to 0.09375
- up_weight: bfloat16 [4096, 14336], P(None, 'fsdp'), may hold values from -0.09375 to 0.09375
- down_weight: bfloat16 [14336, 4096], P('fsdp'), may hold values from -0.046875 to 0.046875
- span_index: bfloat16 [65536, 4096], P(('dp', 'fsdp')), may hold values from -6 to 6
- positive_keys: bfloat16 [1024, 4096], P(('dp', 'fsdp')), may hold values from -6 to 6
- request_rows: int32 [128, 128, 8], P(None, ('dp', 'fsdp')), may hold values from 0 to 511, as said below
- request_counts: int32 [128, 128], P(None, ('dp', 'fsdp')), may hold values from 0 to 8, as said below
- negative_slots: int32 [1024, 64], P(('dp', 'fsdp')), may hold values from 0 to 1023, as said below
Outputs:
- query_loss: float32 [1024], P(('dp', 'fsdp'))
- input_grad: bfloat16 [1024, 4096], P('dp', 'fsdp')
- gate_grad: bfloat16 [4096, 14336], P('dp', 'fsdp')
- up_grad: bfloat16 [4096, 14336], P('dp', 'fsdp')
- down_grad: bfloat16 [14336, 4096], P('fsdp', 'dp')
Inputs may be any that keep to these rules, and one draw needn't show every extreme that they name: `request_rows`: entry [r, o, s] is a local row of shard o; it is read only where s < request_counts[r, o]. `request_counts`: for each requesting device r the counts over the 128 shards sum to 512, and some shard gets exactly 8. `negative_slots`: rows q of device r = q // 8; an entry o * 8 + s names slot s of shard o with s < request_counts[r, o]; the 512 entries of a device use each such slot exactly once.
All inputs are finite; a program needn't handle non-finite values.
Results may differ from a plain program's by a relative error of at most 0.017.
Values may be sent and summed in bfloat16 or wider, within the bound.
A program may use at most 128 MiB of HBM per device.

v0:
```python
import jax
import jax.numpy as jnp
from jax import lax
from jax.sharding import PartitionSpec as P

inverse_temp = 50.0
eps = 1e-06
contract_first = (((0,), (0,)), ((), ()))
contract_last = (((1,), (1,)), ((), ()))


def split3(v):
    hi = lax.reduce_precision(v, 8, 7)
    mid = lax.reduce_precision(v - hi, 8, 7)
    return jnp.concatenate([hi, mid, v - hi - mid], axis=0).astype(jnp.bfloat16)


def contrast(top_state, positive_keys, buffer, negative_slots):
    rows = top_state.shape[0]
    slots = buffer.shape[0]
    row_norm = jnp.sqrt(jnp.sum(top_state * top_state, axis=-1) + eps)
    unit_rows = top_state / row_norm[:, None]
    positive = positive_keys.astype(jnp.float32)
    positive_unit = positive / jnp.sqrt(jnp.sum(positive * positive, axis=-1, keepdims=True) + eps)
    positive_score = inverse_temp * jnp.sum(unit_rows * positive_unit, axis=-1)
    wide = buffer.astype(jnp.float32)
    key_scale = lax.rsqrt(jnp.sum(wide * wide, axis=-1) + eps)
    raw = lax.dot_general(
        split3(unit_rows), buffer, contract_last, preferred_element_type=jnp.float32
    )
    raw = raw[:rows] + raw[rows : 2 * rows] + raw[2 * rows :]
    scores = inverse_temp * raw * key_scale[None, :]
    slot_ids = lax.broadcasted_iota(jnp.int32, (1, 1, slots), 2)
    uses = jnp.sum((negative_slots[:, :, None] == slot_ids).astype(jnp.float32), axis=1)
    weights = jnp.where(uses > 0, uses * jnp.exp(scores), 0.0)
    positive_weight = jnp.exp(positive_score)
    exp_total = jnp.sum(weights, axis=-1) + positive_weight
    query_loss = jnp.log(exp_total) - positive_score
    coeffs = weights / exp_total[:, None]
    positive_coeff = positive_weight / exp_total - 1.0
    pull = lax.dot_general(
        split3(coeffs * key_scale[None, :]),
        buffer,
        (((1,), (0,)), ((), ())),
        preferred_element_type=jnp.float32,
    )
    pull = pull[:rows] + pull[rows : 2 * rows] + pull[2 * rows :]
    pull = inverse_temp * (pull + positive_coeff[:, None] * positive_unit)
    inner = jnp.sum(coeffs * scores, axis=-1) + positive_coeff * positive_score
    head_grad = ((pull - inner[:, None] * unit_rows) / row_norm[:, None]).astype(jnp.bfloat16)
    return (query_loss, head_grad)


def shards(
    mlp_input,
    residual_in,
    gate_weight,
    up_weight,
    down_weight,
    span_index,
    positive_keys,
    request_rows,
    request_counts,
    negative_slots,
):
    owners = lax.axis_size("dp") * lax.axis_size("fsdp")
    slot_cap = request_rows.shape[2]
    width = span_index.shape[1]
    row_table = request_rows[:, 0, :]
    live = lax.broadcasted_iota(jnp.int32, row_table.shape, 1) < request_counts
    wanted = jnp.where(live, row_table, -1).reshape(-1)
    pick = (wanted[:, None] == lax.broadcasted_iota(jnp.int32, (1, span_index.shape[0]), 1)).astype(
        jnp.bfloat16
    )
    picked = jnp.dot(pick, span_index, preferred_element_type=jnp.bfloat16)
    buffer = lax.all_to_all(
        picked.reshape(owners, slot_cap, width),
        ("dp", "fsdp"),
        split_axis=0,
        concat_axis=0,
        tiled=True,
    ).reshape(owners * slot_cap, width)
    whole_input = lax.all_gather(mlp_input, "fsdp", axis=1, tiled=True)
    gate_act = jnp.dot(whole_input, gate_weight, preferred_element_type=jnp.float32)
    up_act = jnp.dot(whole_input, up_weight, preferred_element_type=jnp.float32)
    sigmoid_gate = jax.nn.sigmoid(gate_act)
    silu_gate = gate_act * sigmoid_gate
    hidden = (silu_gate * up_act).astype(jnp.bfloat16)
    branch = lax.psum_scatter(
        jnp.dot(hidden, down_weight, preferred_element_type=jnp.float32).astype(jnp.bfloat16),
        "fsdp",
        scatter_dimension=0,
        tiled=True,
    ).astype(jnp.float32)
    top_state = branch + residual_in.astype(jnp.float32)
    all_hidden = lax.all_gather(hidden, "dp", axis=0, tiled=True)
    input_cols = lax.all_to_all(whole_input, "dp", split_axis=1, concat_axis=0, tiled=True)
    query_loss, head_grad = contrast(top_state, positive_keys, buffer, negative_slots)
    gathered_grad = lax.all_gather(head_grad, "fsdp", axis=0, tiled=True)
    hidden_grad = lax.dot_general(
        gathered_grad, down_weight, contract_last, preferred_element_type=jnp.float32
    )
    silu_slope = sigmoid_gate * (1.0 + gate_act * (1.0 - sigmoid_gate))
    gate_grad_act = (hidden_grad * up_act * silu_slope).astype(jnp.bfloat16)
    up_grad_act = (hidden_grad * silu_gate).astype(jnp.bfloat16)
    both_acts = lax.all_gather(
        jnp.concatenate([gate_grad_act, up_grad_act], axis=1), "dp", axis=0, tiled=True
    )
    input_term = lax.dot_general(
        gate_grad_act, gate_weight, contract_last, preferred_element_type=jnp.float32
    ) + lax.dot_general(up_grad_act, up_weight, contract_last, preferred_element_type=jnp.float32)
    input_grad = lax.psum_scatter(
        input_term.astype(jnp.bfloat16), "fsdp", scatter_dimension=1, tiled=True
    )
    head_cols = lax.all_to_all(gathered_grad, "dp", split_axis=1, concat_axis=0, tiled=True)
    down_grad = lax.dot_general(
        all_hidden, head_cols, contract_first, preferred_element_type=jnp.float32
    ).astype(jnp.bfloat16)
    units = gate_weight.shape[1]
    gate_grad = lax.dot_general(
        input_cols, both_acts[:, :units], contract_first, preferred_element_type=jnp.float32
    ).astype(jnp.bfloat16)
    up_grad = lax.dot_general(
        input_cols, both_acts[:, units:], contract_first, preferred_element_type=jnp.float32
    ).astype(jnp.bfloat16)
    return (query_loss, input_grad, gate_grad, up_grad, down_grad)


def solution(mesh):
    return jax.shard_map(
        shards,
        mesh=mesh,
        in_specs=(
            P("dp", "fsdp"),
            P(("dp", "fsdp"), None),
            P(None, "fsdp"),
            P(None, "fsdp"),
            P("fsdp", None),
            P(("dp", "fsdp"), None),
            P(("dp", "fsdp"), None),
            P(None, ("dp", "fsdp"), None),
            P(None, ("dp", "fsdp")),
            P(("dp", "fsdp"), None),
        ),
        out_specs=(
            P(("dp", "fsdp")),
            P("dp", "fsdp"),
            P("dp", "fsdp"),
            P("dp", "fsdp"),
            P("fsdp", "dp"),
        ),
        check_vma=False,
    )
```

profile of v0, /device:TPU:0, one launch (start us, length us, event | category | flops | bytes accessed | tf_op | source)
XLA Modules:
  0.0 431.6 jit_solution(6093604471115959801)
XLA Ops:
  10.6 9.0 %convolution_bitcast_fusion = bf16[128,8,4096]{2,1,0:T(8,128)(2,1)} fusion(bf16[512,4096]{1,0:T(8,128)(2,1)} %param.15, s32[1024]{0:T(1024)S(1)} %broadcast_select_fusion), kind=kOutput, calls=%fused_computation.5 | convolution fusion | flops 4295491584 | bytes 12587008 | tf_op jit(solution)/shard_map/dot_general | solution.py:75
  19.6 11.7 %all-to-all-start = ((bf16[128,8,4096]{2,1,0:T(8,128)(2,1)}), bf16[128,8,4096]{2,1,0:T(8,128)(2,1)}, u32[]{:S(2)}, u32[]{:S(2)}) async-start(bf16[128,8,4096]{2,1,0:T(8,128)(2,1)} %convolution_bitcast_fusion), calls=%async_computation.1 | async-start | bytes 16777216 | tf_op jit(solution)/shard_map/all_to_all | solution.py:76
  31.3 106.6 %all-gather.4.cloned.1.call-done = bf16[256,4096]{0,1:T(8,128)(2,1)} async-done(((bf16[256,128]{0,1:T(8,128)(2,1)}), bf16[256,4096]{0,1:T(8,128)(2,1)}) %all-gather.4.cloned.1.call-update) | async-done | bytes 2097168 | tf_op jit(solution)/shard_map/all_gather | solution.py:83
  137.9 4.0 fusion.36
  141.9 2.9 multiply_convert_fusion.2
  144.8 2.6 convolution_convert_fusion
  148.1 77.2 %reduce-scatter.5.cloned.1.call-done = bf16[8,4096]{1,0:T(8,128)(2,1)} async-done(((bf16[256,4096]{1,0:T(8,128)(2,1)}), bf16[8,4096]{1,0:T(8,128)(2,1)}) %reduce-scatter.5.cloned.1.call-update) | async-done | bytes 65552 | tf_op jit(solution)/shard_map/reduce_scatter | solution.py:89
  227.4 5.1 %multiply_reduce_fusion = f32[128,8]{1,0:T(8,128)S(1)} fusion(bf16[128,8,4096]{2,1,0:T(8,128)(2,1)} %all-to-all-done), kind=kLoop, calls=%fused_computation | loop fusion | flops 12581888 | bytes 8392704 | tf_op jit(solution)/shard_map/reduce_sum | solution.py:27
  232.7 5.7 %fusion.2 = f32[24,1024]{1,0:T(8,128)S(1)} fusion(bf16[128,8,4096]{2,1,0:T(8,128)(2,1)} %all-to-all-done, bf16[8,4096]{1,0:T(8,128)(2,1)S(1)} %get-tuple-element.16, bf16[8,4096]{1,0:T(8,128)(2,1)S(1)} %get-tuple-element.14, bf16[8,4096]{1,0:T(8,128)(2,1)S(1)} %get-tuple-element.13), kind=kOutput, calls=%fused_computation.3 | convolution fusion | flops 201916416 | bytes 8683520 | tf_op jit(solution)/shard_map/dot_general | solution.py:28
  239.2 4.6 %fusion = f32[24,4096]{1,0:T(8,128)S(1)} fusion(bf16[128,8,4096]{2,1,0:T(8,128)(2,1)} %all-to-all-done, bf16[8,1024]{1,0:T(8,128)(2,1)S(1)} %get-tuple-element.19, bf16[8,1024]{1,0:T(8,128)(2,1)S(1)} %get-tuple-element.18, bf16[8,1024]{1,0:T(8,128)(2,1)S(1)} %get-tuple-element.17), kind=kOutput, calls=%fused_computation.1 | convolution fusion | flops 201474048 | bytes 8830976 | tf_op jit(solution)/shard_map/dot_general | solution.py:41
  244.9 43.1 %all-gather.6.cloned.1.call-done = bf16[256,4096]{1,0:T(8,128)(2,1)} async-done(((bf16[8,4096]{1,0:T(8,128)(2,1)}), bf16[256,4096]{1,0:T(8,128)(2,1)}) %all-gather.6.cloned.1.call-update) | async-done | bytes 2097168 | tf_op jit(solution)/shard_map/all_gather | solution.py:99
  288.0 3.9 multiply_convert_fusion
  292.7 4.5 %all-to-all-start.1 = ((bf16[256,4,1024]{0,2,1:T(8,128)(2,1)}), bf16[256,4,1024]{0,2,1:T(8,128)(2,1)}, u32[]{:S(2)}, u32[]{:S(2)}) async-start(bf16[256,4,1024]{0,2,1:T(8,128)(2,1)} %bitcast.3), calls=%async_computation.2 | async-start | bytes 4194304 | tf_op jit(solution)/shard_map/all_to_all | solution.py:97
  297.2 3.5 fusion.35
  302.1 2.5 copy.29
  304.6 3.2 copy.33
  307.8 26.5 %all-to-all-done.1 = bf16[256,4,1024]{0,2,1:T(8,128)(2,1)} async-done(((bf16[256,4,1024]{0,2,1:T(8,128)(2,1)}), bf16[256,4,1024]{0,2,1:T(8,128)(2,1)}, u32[]{:S(2)}, u32[]{:S(2)}) %all-to-all-start.1) | async-done | bytes 2097184 | tf_op jit(solution)/shard_map/all_to_all | solution.py:97
  334.3 5.2 %all-to-all-start.2 = ((bf16[256,4,1024]{2,0,1:T(8,128)(2,1)}), bf16[256,4,1024]{2,0,1:T(8,128)(2,1)}, u32[]{:S(2)}, u32[]{:S(2)}) async-start(bf16[256,4,1024]{2,0,1:T(8,128)(2,1)} %bitcast.42), calls=%async_computation.3 | async-start | bytes 4194304 | tf_op jit(solution)/shard_map/all_to_all | solution.py:115
  339.4 35.8 %all_gather.15 = bf16[1024,448]{0,1:T(8,128)(2,1)S(1)} all-gather(bf16[256,448]{0,1:T(8,128)(2,1)S(1)} %get-tuple-element.21), channel_id=1, replica_groups=mesh['dp'=4,'fsdp'=32] {'dp'}, dimensions={0}, use_global_device_ids=true | all-gather | bytes 1146880 | tf_op jit(solution)/shard_map/all_gather | solution.py:96
  375.3 3.0 copy.27
  378.3 3.6 convolution_convert_fusion.1
  382.0 3.4 fusion.5
  385.3 2.1 fusion.6
  387.4 36.1 %reduce-scatter.7.cloned.1.call-done = bf16[128,256]{1,0:T(8,128)(2,1)} async-done(((bf16[4096,256]{1,0:T(8,128)(2,1)}), bf16[128,256]{1,0:T(8,128)(2,1)}) %reduce-scatter.7.cloned.1.call-update) | async-done | bytes 65552
  (53 shorter events, 12.0 us)
Async XLA Ops:
  7.2 130.7 %all-gather.4.cloned.1.call-start = ((), (), s32[]{:S(2)}) async-start(), calls=%async_computation.5 | async-start | bytes 2162688 | tf_op jit(solution)/shard_map/all_gather | solution.py:83
  19.6 207.9 %all-to-all-start = ((bf16[128,8,4096]{2,1,0:T(8,128)(2,1)}), bf16[128,8,4096]{2,1,0:T(8,128)(2,1)}, u32[]{:S(2)}, u32[]{:S(2)}) async-start(bf16[128,8,4096]{2,1,0:T(8,128)(2,1)} %convolution_bitcast_fusion), calls=%async_computation.1 | async-start | bytes 16777216 | tf_op jit(solution)/shard_map/all_to_all | solution.py:76
  31.3 194.1 %reduce-scatter.5.cloned.1.call-start = ((), (), s32[]{:S(2)}) async-start(), calls=%async_computation.6 | async-start | bytes 2162688 | tf_op jit(solution)/shard_map/reduce_scatter | solution.py:89
  137.9 4.0 copy-start.1
  141.9 2.9 copy-start
  144.8 2.7 copy-start.4
  144.8 2.9 copy-start.6
  144.8 80.6 %copy-start.3 = (bf16[8,4096]{1,0:T(8,128)(2,1)S(1)}, bf16[8,4096]{1,0:T(8,128)(2,1)}, u32[]{:S(2)}) copy-start(bf16[8,4096]{1,0:T(8,128)(2,1)} %param.11) | copy-start | bytes 196612
  147.5 140.5 %all-gather.6.cloned.1.call-start = ((), (), s32[]{:S(2)}) async-start(), calls=%async_computation.7 | async-start | bytes 2162688 | tf_op jit(solution)/shard_map/all_gather | solution.py:99
  239.2 4.6 %copy-start.5 = (bf16[8,4096]{1,0:T(8,128)(2,1)S(1)}, bf16[8,4096]{1,0:T(8,128)(2,1)}, u32[]{:S(2)}) copy-start(bf16[8,4096]{1,0:T(8,128)(2,1)} %reduce-scatter.5.cloned.1.call-done) | copy-start | bytes 196612
  244.6 137.3 %all-gather.8.cloned.1.call-start = ((), (), s32[]{:S(2)}) async-start(), calls=%async_computation.8 | async-start | bytes 2293760 | tf_op jit(solution)/shard_map/all_gather | solution.py:106
  292.7 41.6 %all-to-all-start.1 = ((bf16[256,4,1024]{0,2,1:T(8,128)(2,1)}), bf16[256,4,1024]{0,2,1:T(8,128)(2,1)}, u32[]{:S(2)}, u32[]{:S(2)}) async-start(bf16[256,4,1024]{0,2,1:T(8,128)(2,1)} %bitcast.3), calls=%async_computation.2 | async-start | bytes 4194304 | tf_op jit(solution)/shard_map/all_to_all | solution.py:97
  297.2 126.3 %reduce-scatter.7.cloned.1.call-start = ((), (), s32[]{:S(2)}) async-start(), calls=%async_computation.9 | async-start | bytes 2162688
  297.2 3.5 copy-start.2
  334.3 44.0 %all-to-all-start.2 = ((bf16[256,4,1024]{2,0,1:T(8,128)(2,1)}), bf16[256,4,1024]{2,0,1:T(8,128)(2,1)}, u32[]{:S(2)}, u32[]{:S(2)}) async-start(bf16[256,4,1024]{2,0,1:T(8,128)(2,1)} %bitcast.42), calls=%async_computation.3 | async-start | bytes 4194304 | tf_op jit(solution)/shard_map/all_to_all | solution.py:115
  382.0 3.4 copy-start.7
Sparse Core Ops, SparseCore 0:
  10.8 127.0 all-gather.3
  147.6 77.7 reduce-scatter.4
  244.8 43.1 all-gather.5
  292.8 46.3 all-gather.7
  342.5 80.8 reduce-scatter.6
where the time goes:
time: 432 us
  waiting for transfers between devices  290 us (67%)
  matrix products  46.6 us (11%)
  blocking collectives  35.8 us (8%)
  starting transfers between devices  21.7 us (5%)
  between operations  14 us (3%)
  local copies, waits for them, and re-layouts  12.9 us (3%)
  other arithmetic  11 us (3%)
    all_gather x1, waiting for transfers between devices, shards(): whole_input = lax.all_gather(mlp_input, 'fsdp', axis=1, tiled=True)  107 us
    reduce_scatter x1, waiting for transfers between devices, shards(): lax.psum_scatter(jnp.dot(hidden, down_weight, preferred_element_type=jnp....  77.2 us
    all_gather x1, waiting for transfers between devices, shards(): gathered_grad = lax.all_gather(head_grad, 'fsdp', axis=0, tiled=True)  43.1 us
    unnamed x6, waiting for transfers between devices  36.2 us
    all_gather x1, blocking collectives, shards(): all_hidden = lax.all_gather(hidden, 'dp', axis=0, tiled=True)  35.8 us
    all_to_all x1, waiting for transfers between devices, shards(): lax.all_to_all(whole_input, 'dp', split_axis=1, concat_axis=0, tiled=True)  26.5 us
    all_to_all x1, starting transfers between devices, shards(): lax.all_to_all(picked.reshape(owners, slot_cap, width), ('dp', 'fsdp'), s...  11.7 us
    dot_general x1, matrix products, shards(): picked = jnp.dot(pick, span_index, preferred_element_type=jnp.bfloat16)  9.02 us
  transfers between devices with their start and end apart: 8, of which 5 were waited for; matrix products, arithmetic and copies ran while one was open for 11% of the time, Pallas kernels for 0%

commit v1 on v0

--- a/solution.py
+++ b/solution.py
@@ -96,7 +96,9 @@
     all_hidden = lax.all_gather(hidden, "dp", axis=0, tiled=True)
     input_cols = lax.all_to_all(whole_input, "dp", split_axis=1, concat_axis=0, tiled=True)
     query_loss, head_grad = contrast(top_state, positive_keys, buffer, negative_slots)
-    gathered_grad = lax.all_gather(head_grad, "fsdp", axis=0, tiled=True)
+    gathered_grad = jnp.concatenate(
+        lax.all_to_all(jnp.stack([head_grad] * lax.axis_size("fsdp")), "fsdp", 0, 0), axis=0
+    )
     hidden_grad = lax.dot_general(
         gathered_grad, down_weight, contract_last, preferred_element_type=jnp.float32
     )

time: 432 us -> 419 us (0.970)
  waiting for transfers between devices: 290 us -> 239 us
  blocking collectives: 35.8 us -> 70.2 us
  local copies, waits for them, and re-layouts: 12.9 us -> 18.6 us
    all_gather x1 -> x0, waiting for transfers between devices: 43.1 us -> none  [shards(): gathered_grad = lax.all_gather(head_grad, 'fsdp', axis=0, tiled=True)]
    all_to_all x0 -> x1, blocking collectives: none -> 33.9 us  [shards(): lax.all_to_all(jnp.stack([head_grad] * lax.axis_size('fsdp')), 'fsdp', 0, 0)]
    unnamed x6 -> x5, waiting for transfers between devices: 36.2 us -> 32.6 us
    unnamed x20 -> x26, local copies, waits for them, and re-layouts: 6.45 us -> 8.7 us
  transfers between devices with their start and end apart: 8 -> 7, of which waited for: 5 -> 4; matrix products, arithmetic and copies ran while one was open for 11% -> 11% of each run, Pallas kernels for 0% -> 0%
where the time goes in v1:
time: 419 us; the launch traced here: 418 us
  waiting for transfers between devices  239 us (57%)
  blocking collectives  70.2 us (17%)
  matrix products  44 us (11%)
  starting transfers between devices  21.1 us (5%)
  local copies, waits for them, and re-layouts  18.6 us (4%)
  between operations  14 us (3%)
  other arithmetic  10.4 us (2%)
    all_gather x1, waiting for transfers between devices, shards(): whole_input = lax.all_gather(mlp_input, 'fsdp', axis=1, tiled=True)  107 us
    reduce_scatter x1, waiting for transfers between devices, shards(): lax.psum_scatter(jnp.dot(hidden, down_weight, preferred_element_type=jnp....  76.5 us
    all_gather x1, blocking collectives, shards(): all_hidden = lax.all_gather(hidden, 'dp', axis=0, tiled=True)  36.4 us
    all_to_all x1, blocking collectives, shards(): lax.all_to_all(jnp.stack([head_grad] * lax.axis_size('fsdp')), 'fsdp', 0, 0)  33.9 us
    unnamed x5, waiting for transfers between devices  32.6 us
    all_to_all x1, waiting for transfers between devices, shards(): lax.all_to_all(whole_input, 'dp', split_axis=1, concat_axis=0, tiled=True)  23.7 us
    all_to_all x1, starting transfers between devices, shards(): lax.all_to_all(picked.reshape(owners, slot_cap, width), ('dp', 'fsdp'), s...  11.7 us
    dot_general x1, matrix products, shards(): picked = jnp.dot(pick, span_index, preferred_element_type=jnp.bfloat16)  9.02 us
  transfers between devices with their start and end apart: 7, of which 4 were waited for; matrix products, arithmetic and copies ran while one was open for 11% of the time, Pallas kernels for 0%

profile of v1, /device:TPU:0, one launch (start us, length us, event | category | flops | bytes accessed | tf_op | source)
XLA Modules:
  0.0 417.6 jit_solution(5713844455338281506)
XLA Ops:
  10.6 9.0 %convolution_bitcast_fusion = bf16[128,8,4096]{2,1,0:T(8,128)(2,1)} fusion(bf16[512,4096]{1,0:T(8,128)(2,1)} %param.15, s32[1024]{0:T(1024)S(1)} %broadcast_select_fusion), kind=kOutput, calls=%fused_computation.5 | convolution fusion | flops 4295491584 | bytes 12587008 | tf_op jit(solution)/shard_map/dot_general | solution.py:75
  19.6 11.7 %all-to-all-start = ((bf16[128,8,4096]{2,1,0:T(8,128)(2,1)}), bf16[128,8,4096]{2,1,0:T(8,128)(2,1)}, u32[]{:S(2)}, u32[]{:S(2)}) async-start(bf16[128,8,4096]{2,1,0:T(8,128)(2,1)} %convolution_bitcast_fusion), calls=%async_computation.1 | async-start | bytes 16777216 | tf_op jit(solution)/shard_map/all_to_all | solution.py:76
  31.3 106.6 %all-gather.3.cloned.1.call-done = bf16[256,4096]{0,1:T(8,128)(2,1)} async-done(((bf16[256,128]{0,1:T(8,128)(2,1)}), bf16[256,4096]{0,1:T(8,128)(2,1)}) %all-gather.3.cloned.1.call-update) | async-done | bytes 2097168 | tf_op jit(solution)/shard_map/all_gather | solution.py:83
  137.9 4.0 fusion.38
  141.9 2.9 multiply_convert_fusion.2
  144.8 2.6 convolution_convert_fusion
  148.9 76.5 %reduce-scatter.5.cloned.1.call-done = bf16[8,4096]{1,0:T(8,128)(2,1)} async-done(((bf16[256,4096]{1,0:T(8,128)(2,1)}), bf16[8,4096]{1,0:T(8,128)(2,1)}) %reduce-scatter.5.cloned.1.call-update) | async-done | bytes 65552 | tf_op jit(solution)/shard_map/reduce_scatter | solution.py:89
  227.4 5.1 %multiply_reduce_fusion = f32[128,8]{1,0:T(8,128)S(1)} fusion(bf16[128,8,4096]{2,1,0:T(8,128)(2,1)} %all-to-all-done), kind=kLoop, calls=%fused_computation | loop fusion | flops 12581888 | bytes 8392704 | tf_op jit(solution)/shard_map/reduce_sum | solution.py:27
  232.6 5.7 %fusion.2 = f32[24,1024]{1,0:T(8,128)S(1)} fusion(bf16[128,8,4096]{2,1,0:T(8,128)(2,1)} %all-to-all-done, bf16[8,4096]{1,0:T(8,128)(2,1)S(1)} %get-tuple-element.16, bf16[8,4096]{1,0:T(8,128)(2,1)S(1)} %get-tuple-element.14, bf16[8,4096]{1,0:T(8,128)(2,1)S(1)} %get-tuple-element.13), kind=kOutput, calls=%fused_computation.3 | convolution fusion | flops 201916416 | bytes 8683520 | tf_op jit(solution)/shard_map/dot_general | solution.py:28
  239.2 4.6 %fusion = f32[24,4096]{1,0:T(8,128)S(1)} fusion(bf16[128,8,4096]{2,1,0:T(8,128)(2,1)} %all-to-all-done, bf16[8,1024]{1,0:T(8,128)(2,1)S(1)} %get-tuple-element.19, bf16[8,1024]{1,0:T(8,128)(2,1)S(1)} %get-tuple-element.18, bf16[8,1024]{1,0:T(8,128)(2,1)S(1)} %get-tuple-element.17), kind=kOutput, calls=%fused_computation.1 | convolution fusion | flops 201474048 | bytes 8830976 | tf_op jit(solution)/shard_map/dot_general | solution.py:41
  244.2 33.9 %all_to_all.48 = bf16[32,8,4096]{2,1,0:T(8,128)(2,1)S(1)} all-to-all(bf16[32,8,4096]{2,1,0:T(8,128)(2,1)S(1)} %stack.2), channel_id=1, replica_groups=mesh['dp'=4,'fsdp'=32] {'fsdp'}, dimensions={0} | all-to-all | bytes 4194304 | tf_op jit(solution)/shard_map/all_to_all | solution.py:100
  280.2 4.5 %all-to-all-start.2 = ((bf16[256,4,1024]{0,2,1:T(8,128)(2,1)}), bf16[256,4,1024]{0,2,1:T(8,128)(2,1)}, u32[]{:S(2)}, u32[]{:S(2)}) async-start(bf16[256,4,1024]{0,2,1:T(8,128)(2,1)} %bitcast.4), calls=%async_computation.3 | async-start | bytes 4194304 | tf_op jit(solution)/shard_map/all_to_all | solution.py:97
  284.7 3.6 fusion.37
  289.7 2.5 copy.28
  293.8 2.8 all_to_all.40
  296.6 3.5 copy.27
  300.1 23.7 %all-to-all-done.2 = bf16[256,4,1024]{0,2,1:T(8,128)(2,1)} async-done(((bf16[256,4,1024]{0,2,1:T(8,128)(2,1)}), bf16[256,4,1024]{0,2,1:T(8,128)(2,1)}, u32[]{:S(2)}, u32[]{:S(2)}) %all-to-all-start.2) | async-done | bytes 2097184 | tf_op jit(solution)/shard_map/all_to_all | solution.py:97
  323.9 4.6 %all-to-all-start.3 = ((bf16[256,4,1024]{2,0,1:T(8,128)(2,1)}), bf16[256,4,1024]{2,0,1:T(8,128)(2,1)}, u32[]{:S(2)}, u32[]{:S(2)}) async-start(bf16[256,4,1024]{2,0,1:T(8,128)(2,1)} %copy.27), calls=%async_computation.4 | async-start | bytes 4194304 | tf_op jit(solution)/shard_map/all_to_all | solution.py:117
  328.5 36.4 %all_gather.11 = bf16[1024,448]{0,1:T(8,128)(2,1)S(1)} all-gather(bf16[256,448]{0,1:T(8,128)(2,1)S(1)} %get-tuple-element.21), channel_id=1, replica_groups=mesh['dp'=4,'fsdp'=32] {'dp'}, dimensions={0}, use_global_device_ids=true | all-gather | bytes 1146880 | tf_op jit(solution)/shard_map/all_gather | solution.py:96
  364.9 3.0 copy.26
  367.9 3.6 convolution_convert_fusion.1
  371.5 3.4 fusion.7
  374.9 2.1 fusion.8
  376.9 32.5 %reduce-scatter.7.cloned.1.call-done = bf16[128,256]{1,0:T(8,128)(2,1)} async-done(((bf16[4096,256]{1,0:T(8,128)(2,1)}), bf16[128,256]{1,0:T(8,128)(2,1)}) %reduce-scatter.7.cloned.1.call-update) | async-done | bytes 65552
  (59 shorter events, 15.0 us)
Async XLA Ops:
  7.2 130.7 %all-gather.3.cloned.1.call-start = ((), (), s32[]{:S(2)}) async-start(), calls=%async_computation.6 | async-start | bytes 2162688 | tf_op jit(solution)/shard_map/all_gather | solution.py:83
  19.6 207.8 %all-to-all-start = ((bf16[128,8,4096]{2,1,0:T(8,128)(2,1)}), bf16[128,8,4096]{2,1,0:T(8,128)(2,1)}, u32[]{:S(2)}, u32[]{:S(2)}) async-start(bf16[128,8,4096]{2,1,0:T(8,128)(2,1)} %convolution_bitcast_fusion), calls=%async_computation.1 | async-start | bytes 16777216 | tf_op jit(solution)/shard_map/all_to_all | solution.py:76
  31.3 194.1 %reduce-scatter.5.cloned.1.call-start = ((), (), s32[]{:S(2)}) async-start(), calls=%async_computation.7 | async-start | bytes 2162688 | tf_op jit(solution)/shard_map/reduce_scatter | solution.py:89
  137.9 4.0 copy-start.4
  141.9 2.9 copy-start.2
  147.4 0.8 copy-start.7
  147.4 1.0 copy-start.9
  147.4 77.9 %copy-start.6 = (bf16[8,4096]{1,0:T(8,128)(2,1)S(1)}, bf16[8,4096]{1,0:T(8,128)(2,1)}, u32[]{:S(2)}) copy-start(bf16[8,4096]{1,0:T(8,128)(2,1)} %param.11) | copy-start | bytes 196612
  147.4 224.1 %all-gather.5.cloned.1.call-start = ((), (), s32[]{:S(2)}) async-start(), calls=%async_computation.8 | async-start | bytes 2293760 | tf_op jit(solution)/shard_map/all_gather | solution.py:108
  239.2 4.6 %copy-start.8 = (bf16[8,4096]{1,0:T(8,128)(2,1)S(1)}, bf16[8,4096]{1,0:T(8,128)(2,1)}, u32[]{:S(2)}) copy-start(bf16[8,4096]{1,0:T(8,128)(2,1)} %reduce-scatter.5.cloned.1.call-done) | copy-start | bytes 196612
  244.2 33.9 %copy-start.3 = (bf16[448,4096]{1,0:T(8,128)(2,1)S(1)}, bf16[448,4096]{1,0:T(8,128)(2,1)}, u32[]{:S(2)}) copy-start(bf16[448,4096]{1,0:T(8,128)(2,1)} %param.14) | copy-start | bytes 11010052
  278.1 1.3 copy-start
  280.2 43.7 %all-to-all-start.2 = ((bf16[256,4,1024]{0,2,1:T(8,128)(2,1)}), bf16[256,4,1024]{0,2,1:T(8,128)(2,1)}, u32[]{:S(2)}, u32[]{:S(2)}) async-start(bf16[256,4,1024]{0,2,1:T(8,128)(2,1)} %bitcast.4), calls=%async_computation.3 | async-start | bytes 4194304 | tf_op jit(solution)/shard_map/all_to_all | solution.py:97
  284.7 124.8 %reduce-scatter.7.cloned.1.call-start = ((), (), s32[]{:S(2)}) async-start(), calls=%async_computation.9 | async-start | bytes 2162688
  284.7 3.6 copy-start.5
  292.2 1.6 copy-start.1
  323.9 44.0 %all-to-all-start.3 = ((bf16[256,4,1024]{2,0,1:T(8,128)(2,1)}), bf16[256,4,1024]{2,0,1:T(8,128)(2,1)}, u32[]{:S(2)}, u32[]{:S(2)}) async-start(bf16[256,4,1024]{2,0,1:T(8,128)(2,1)} %copy.27), calls=%async_computation.4 | async-start | bytes 4194304 | tf_op jit(solution)/shard_map/all_to_all | solution.py:117
  371.5 3.4 copy-start.10
Sparse Core Ops, SparseCore 0:
  10.8 127.0 all-gather.2
  147.6 77.7 reduce-scatter.4
  280.3 46.1 all-gather.4
  329.9 79.5 reduce-scatter.6
